TPU v7x, 32 devices: a whole 2x2x4 slice. The times are simulated.
32 devices in a mesh: groups: 2 (over y), row: 4 (over z), col: 4 (over x, core).
Axes of the slice: x: 2, y: 2, z: 4, core: 2. Of those that a mesh axis runs over, the one named last changes fastest.
Arguments:
- green_starting_blocks: float32 [4, 128, 2048], P('groups', None, ('row', 'col')), parts along dimension 0, may hold values from -3 to 3
- fit_vectors: bfloat16 [256, 4096], P('groups'), parts along dimension 0, may hold values from -0.75 to 0.75
- history: bfloat16 [4, 2048, 2048], P('groups', 'row', 'col'), parts along dimension 0, may hold values from -0.125 to 0.125
Outputs:
- green_final: float32 [4, 128, 2048], P('groups', None, ('row', 'col')), parts along dimension 0
There are 2 independent parts, one for each index of `groups`. A program takes and returns all parts, laid end to end along the dimension named above; each array names one. Nothing has to cross between parts.
All inputs are finite; a program needn't handle non-finite values.
Results may differ from a plain program's by a relative error of at most 0.03.
Values may be sent and summed in bfloat16 or wider, within the bound.
A program may use at most 128 MiB of HBM per device.

v0:
```python
import jax
import jax.numpy as jnp
from jax import lax
from jax.sharding import PartitionSpec as P

NO = 64
NEW = 2
ITERS = 2


def pair_self_energy(pair_blocks, fit_vectors):
    pair_count = pair_blocks.shape[1]
    orbitals = pair_blocks.shape[2]
    aux_count = fit_vectors.shape[0]
    lowered = pair_blocks.astype(jnp.bfloat16)
    fit_basis = fit_vectors.reshape(aux_count * orbitals, orbitals)
    inner_side = jnp.transpose(lowered, (2, 0, 1, 3)).reshape(orbitals, 2 * pair_count * orbitals)
    left_prod = jnp.dot(fit_basis, inner_side, preferred_element_type=jnp.float32).astype(
        jnp.bfloat16
    )
    left_prod = left_prod.reshape(aux_count, orbitals, 2, pair_count, orbitals)
    fit_turned = jnp.transpose(
        fit_vectors.reshape(aux_count, orbitals, orbitals), (1, 0, 2)
    ).reshape(orbitals, aux_count * orbitals)
    right_prod = jnp.dot(
        lowered.reshape(2 * pair_count * orbitals, orbitals),
        fit_turned,
        preferred_element_type=jnp.float32,
    ).astype(jnp.bfloat16)
    right_prod = right_prod.reshape(2, pair_count, orbitals, aux_count, orbitals)
    bubble = (
        jnp.einsum("picnk,cniqk->npq", left_prod, right_prod, preferred_element_type=jnp.float32)
        / orbitals
    )
    bubble = bubble.astype(jnp.bfloat16)
    screened = jnp.einsum(
        "npq,qm->npm", bubble, fit_vectors, preferred_element_type=jnp.float32
    ).astype(jnp.bfloat16)
    screened = screened.reshape(pair_count, aux_count, orbitals, orbitals)
    scale_factor = (aux_count * orbitals) ** (-0.5)
    energy = (
        jnp.einsum("picnl,nplj->cnij", left_prod, screened, preferred_element_type=jnp.float32)
        * scale_factor
    )
    return energy.astype(jnp.bfloat16)


def local(green_starting_blocks, fit_vectors, history):
    row_count = green_starting_blocks.shape[1]
    span_cols = green_starting_blocks.shape[2]
    local_times = span_cols // NO
    row_devices = lax.axis_size("row")
    col_devices = lax.axis_size("col")
    row_ratio = row_devices // col_devices
    green_current = green_starting_blocks
    for iteration in range(ITERS):
        pair_blocks = green_current.reshape(2, NEW, NO, local_times, NO).transpose(0, 1, 3, 2, 4)
        pair_blocks = pair_blocks.reshape(2, NEW * local_times, NO, NO)
        energies = pair_self_energy(pair_blocks, fit_vectors)
        self_energy = energies.reshape(2, NEW, local_times, NO, NO).transpose(0, 1, 3, 2, 4)
        self_energy = self_energy.reshape(2, row_count, span_cols)
        segment = lax.all_gather(self_energy, "col", axis=2, tiled=True)
        seg_width = segment.shape[2]
        stacked = segment.reshape(2 * row_count, seg_width)
        real_rows = history[0]
        imag_rows = history[1]
        real_half = jnp.dot(stacked, real_rows, preferred_element_type=jnp.float32)
        imaginary_half = jnp.dot(stacked, imag_rows, preferred_element_type=jnp.float32)
        totals = (
            real_half[:row_count] - imaginary_half[row_count:],
            imaginary_half[:row_count] + real_half[row_count:],
        )
        partial_value = jnp.stack(totals)
        shaped = partial_value.reshape(2, row_count, 1, row_ratio, col_devices, span_cols)
        shuffled = lax.all_to_all(
            shaped.astype(jnp.bfloat16), "col", split_axis=4, concat_axis=2, tiled=True
        ).astype(shaped.dtype)
        shuffled = shuffled.reshape(2, row_count, row_devices, span_cols)
        summed = lax.psum_scatter(
            shuffled.astype(jnp.bfloat16), "row", scatter_dimension=2, tiled=True
        ).astype(jnp.float32)
        collision = summed.reshape(2, row_count, span_cols)
        green_current = green_starting_blocks + collision
    return green_current


def solution(mesh):
    in_specs = (P("groups", None, ("row", "col")), P("groups", None), P("groups", "row", "col"))
    out_specs = P("groups", None, ("row", "col"))
    return jax.shard_map(local, mesh=mesh, in_specs=in_specs, out_specs=out_specs, check_vma=False)
```

profile of v0, /device:TPU:0, one launch (start us, length us, event | category | flops | bytes accessed | tf_op | source)
XLA Modules:
  0.0 335.3 jit_solution(7470112163291721763)
XLA Ops:
  14.8 3.3 reshape.182
  18.2 5.5 %convolution_convert_fusion.3 = bf16[8192,512]{1,0:T(8,128)(2,1)} fusion(bf16[8192,64]{1,0:T(8,128)(2,1)S(1)} %reshape.178, bf16[64,512]{1,0:T(8,128)(2,1)S(1)} %reshape.179), kind=kOutput, calls=%fused_computation.7 | convolution fusion | flops 541065216 | bytes 9502720 | tf_op jit(solution)/shard_map/dot_general | solution.py:18
  23.7 11.4 %copy.54 = bf16[8192,512]{0,1:T(8,128)(2,1)} copy(bf16[8192,512]{1,0:T(8,128)(2,1)} %convolution_convert_fusion.3) | data formatting | bytes 16777216 | tf_op jit(solution)/shard_map/convert_element_type | solution.py:18
  35.1 23.6 %reshape.180 = bf16[128,64,2,4,64]{1,0,4,3,2:T(8,128)(2,1)} reshape(bf16[8192,512]{0,1:T(8,128)(2,1)} %copy.54) | data formatting | bytes 16777216 | tf_op jit(solution)/shard_map/reshape | solution.py:21
  58.7 5.6 %convolution_convert_fusion.2 = bf16[512,8192]{1,0:T(8,128)(2,1)} fusion(bf16[512,64]{0,1:T(8,128)(2,1)S(1)} %convert_element_type.110, bf16[64,8192]{1,0:T(8,128)(2,1)S(1)} %reshape.182), kind=kOutput, calls=%fused_computation.6 | convolution fusion | flops 541065216 | bytes 9502720 | tf_op jit(solution)/shard_map/dot_general | solution.py:25
  64.3 23.6 %reshape.183 = bf16[2,4,64,128,64]{4,3,2,1,0:T(8,128)(2,1)} reshape(bf16[512,8192]{1,0:T(8,128)(2,1)} %convolution_convert_fusion.2) | data formatting | bytes 16777216 | tf_op jit(solution)/shard_map/reshape | solution.py:30
  87.9 18.9 %copy.59 = bf16[2,4,64,128,64]{3,2,4,1,0:T(8,128)(2,1)} copy(bf16[2,4,64,128,64]{4,3,2,1,0:T(8,128)(2,1)} %reshape.183) | data formatting | bytes 16777216 | tf_op jit(solution)/shard_map/reshape | solution.py:30
  106.8 14.8 %convolution_convert_fusion.5 = bf16[4,128,4096]{2,1,0:T(8,128)(2,1)} fusion(bf16[128,64,2,4,64]{1,0,4,3,2:T(8,128)(2,1)} %reshape.180, bf16[2,4,64,128,64]{3,2,4,1,0:T(8,128)(2,1)} %copy.59, bf16[128,4096]{1,0:T(8,128)(2,1)S(1)} %copy-done), kind=kOutput, calls=%fused_computation.10 | convolution fusion | flops 1612840960 | bytes 22020096 | tf_op jit(solution)/shard_map/npq,qm->npm/dot_general | solution.py:36
  121.6 6.3 %copy.60 = bf16[4,128,4096]{1,2,0:T(8,128)(2,1)} copy(bf16[4,128,4096]{2,1,0:T(8,128)(2,1)} %convolution_convert_fusion.5) | data formatting | bytes 8388608 | tf_op jit(solution)/shard_map/convert_element_type | solution.py:38
  127.9 10.1 %fusion.21 = bf16[4,64,64,2]{2,1,3,0:T(8,128)(2,1)S(1)} fusion(bf16[4,128,64,64,1]{1,3,2,4,0:T(8,128)(2,1)} %bitcast.117, bf16[128,64,2,4,64]{1,0,4,3,2:T(8,128)(2,1)} %reshape.180), kind=kOutput, calls=%fused_computation.21 | convolution fusion | flops 536936448 | bytes 12648448 | tf_op jit(solution)/shard_map/picnl,nplj->cnij/dot_general | solution.py:42
  138.3 7.3 %all_gather.6 = bf16[2,128,512]{2,1,0:T(8,128)(2,1)S(1)} all-gather(bf16[2,128,128]{2,1,0:T(8,128)(2,1)S(1)} %reshape.186), channel_id=1, replica_groups=mesh['groups'=2,'row'=4,'col'=4] {'col'}, dimensions={2}, use_global_device_ids=true | all-gather | bytes 327680 | tf_op jit(solution)/shard_map/all_gather | solution.py:62
  151.6 9.1 %all_to_all.24 = bf16[2,128,1,1,4,128]{5,1,0,3,2,4:T(8,128)(2,1)} all-to-all(bf16[2,128,1,1,4,128]{5,1,0,3,2,4:T(8,128)(2,1)S(1)} %pad_maximum_fusion), channel_id=1, replica_groups=mesh['groups'=2,'row'=4,'col'=4] {'col'}, dimensions={4} | all-to-all | bytes 524288 | tf_op jit(solution)/shard_map/all_to_all | solution.py:75
  160.8 20.5 %reduce-scatter.3.cloned.1.call-done = bf16[2,128,1,128]{3,1,0,2:T(8,128)(2,1)} async-done(((bf16[2,128,4,128]{3,1,0,2:T(8,128)(2,1)}), bf16[2,128,1,128]{3,1,0,2:T(8,128)(2,1)}) %reduce-scatter.3.cloned.1.call-update) | async-done | bytes 65552 | tf_op jit(solution)/shard_map/reduce_scatter | solution.py:79
  184.9 5.6 %fusion.4 = bf16[8192,512]{0,1:T(8,128)(2,1)} fusion(bf16[64,512]{1,0:T(8,128)(2,1)S(1)} %reshape.190, bf16[8192,64]{1,0:T(8,128)(2,1)S(1)} %reshape.178), kind=kOutput, calls=%fused_computation.8 | convolution fusion | flops 541065216 | bytes 9502720 | tf_op jit(solution)/shard_map/dot_general | solution.py:18
  190.6 5.6 %convolution_convert_fusion = bf16[512,8192]{1,0:T(8,128)(2,1)} fusion(bf16[512,64]{0,1:T(8,128)(2,1)S(1)} %copy-done.5, bf16[64,8192]{1,0:T(8,128)(2,1)S(1)} %copy-done.2), kind=kOutput, calls=%fused_computation.4 | convolution fusion | flops 541065216 | bytes 9502720 | tf_op jit(solution)/shard_map/dot_general | solution.py:25
  196.1 23.6 %reshape.191 = bf16[128,64,2,4,64]{1,0,4,3,2:T(8,128)(2,1)} reshape(bf16[8192,512]{0,1:T(8,128)(2,1)} %fusion.4) | data formatting | bytes 16777216 | tf_op jit(solution)/shard_map/reshape | solution.py:21
  219.7 23.6 %reshape.192 = bf16[2,4,64,128,64]{4,3,2,1,0:T(8,128)(2,1)} reshape(bf16[512,8192]{1,0:T(8,128)(2,1)} %convolution_convert_fusion) | data formatting | bytes 16777216 | tf_op jit(solution)/shard_map/reshape | solution.py:30
  243.3 18.8 %copy.69 = bf16[2,4,64,128,64]{3,2,4,1,0:T(8,128)(2,1)} copy(bf16[2,4,64,128,64]{4,3,2,1,0:T(8,128)(2,1)} %reshape.192) | data formatting | bytes 16777216 | tf_op jit(solution)/shard_map/reshape | solution.py:30
  262.1 14.8 %convolution_convert_fusion.4 = bf16[4,128,4096]{2,1,0:T(8,128)(2,1)} fusion(bf16[128,64,2,4,64]{1,0,4,3,2:T(8,128)(2,1)} %reshape.191, bf16[2,4,64,128,64]{3,2,4,1,0:T(8,128)(2,1)} %copy.69, bf16[128,4096]{1,0:T(8,128)(2,1)S(1)} %copy-done), kind=kOutput, calls=%fused_computation.9 | convolution fusion | flops 1612840960 | bytes 22020096 | tf_op jit(solution)/shard_map/npq,qm->npm/dot_general | solution.py:36
  276.9 6.3 %copy.70 = bf16[4,128,4096]{1,2,0:T(8,128)(2,1)} copy(bf16[4,128,4096]{2,1,0:T(8,128)(2,1)} %convolution_convert_fusion.4) | data formatting | bytes 8388608 | tf_op jit(solution)/shard_map/convert_element_type | solution.py:38
  283.3 10.1 %fusion.24 = bf16[4,64,64,2]{2,1,3,0:T(8,128)(2,1)S(1)} fusion(bf16[4,128,64,64,1]{1,3,2,4,0:T(8,128)(2,1)} %bitcast.118, bf16[128,64,2,4,64]{1,0,4,3,2:T(8,128)(2,1)} %reshape.191), kind=kOutput, calls=%fused_computation.22 | convolution fusion | flops 536936448 | bytes 12648448 | tf_op jit(solution)/shard_map/picnl,nplj->cnij/dot_general | solution.py:42
  293.7 5.8 %all_gather.7 = bf16[2,128,512]{2,1,0:T(8,128)(2,1)S(1)} all-gather(bf16[2,128,128]{2,1,0:T(8,128)(2,1)S(1)} %reshape.195), channel_id=1, replica_groups=mesh['groups'=2,'row'=4,'col'=4] {'col'}, dimensions={2}, use_global_device_ids=true | all-gather | bytes 327680 | tf_op jit(solution)/shard_map/all_gather | solution.py:62
  300.4 9.1 %all_to_all.25 = bf16[2,128,1,1,4,128]{5,1,0,3,2,4:T(8,128)(2,1)} all-to-all(bf16[2,128,1,1,4,128]{5,1,0,3,2,4:T(8,128)(2,1)S(1)} %pad_maximum_fusion.1), channel_id=1, replica_groups=mesh['groups'=2,'row'=4,'col'=4] {'col'}, dimensions={4} | all-to-all | bytes 524288 | tf_op jit(solution)/shard_map/all_to_all | solution.py:75
  309.5 17.5 %reduce-scatter.5.cloned.1.call-done = bf16[2,128,1,128]{3,1,0,2:T(8,128)(2,1)} async-done(((bf16[2,128,4,128]{3,1,0,2:T(8,128)(2,1)}), bf16[2,128,1,128]{3,1,0,2:T(8,128)(2,1)}) %reduce-scatter.5.cloned.1.call-update) | async-done | bytes 65552 | tf_op jit(solution)/shard_map/reduce_scatter | solution.py:79
  (54 shorter events, 20.9 us)
Async XLA Ops:
  6.5 174.7 %reduce-scatter.3.cloned.1.call-start = ((), (), s32[]{:S(2)}) async-start(), calls=%async_computation.4 | async-start | bytes 327680 | tf_op jit(solution)/shard_map/reduce_scatter | solution.py:79
  18.2 40.5 %copy-start.1 = (bf16[64,8192]{1,0:T(8,128)(2,1)}, bf16[64,8192]{1,0:T(8,128)(2,1)S(1)}, u32[]{:S(2)}) copy-start(bf16[64,8192]{1,0:T(8,128)(2,1)S(1)} %reshape.182) | copy-start | bytes 3145732
  87.9 18.9 %copy-start = (bf16[128,4096]{1,0:T(8,128)(2,1)S(1)}, bf16[128,4096]{1,0:T(8,128)(2,1)}, u32[]{:S(2)}) copy-start(bf16[128,4096]{1,0:T(8,128)(2,1)} %param.4) | copy-start | bytes 3145732
  127.9 53.3 %copy-start.4 = (f32[2,128,128]{2,1,0:T(8,128)S(1)}, f32[2,128,128]{2,1,0:T(8,128)}, u32[]{:S(2)}) copy-start(f32[2,128,128]{2,1,0:T(8,128)} %param.3) | copy-start | bytes 393220
  160.7 166.2 %reduce-scatter.5.cloned.1.call-start = ((), (), s32[]{:S(2)}) async-start(), calls=%async_computation.5 | async-start | bytes 327680 | tf_op jit(solution)/shard_map/reduce_scatter | solution.py:79
  184.8 5.8 %copy-start.5 = (bf16[512,64]{0,1:T(8,128)(2,1)S(1)}, bf16[512,64]{0,1:T(8,128)(2,1)}, u32[]{:S(2)}) copy-start(bf16[512,64]{0,1:T(8,128)(2,1)} %convert_element_type.122) | copy-start | bytes 196612
  184.9 5.6 %copy-start.2 = (bf16[64,8192]{1,0:T(8,128)(2,1)S(1)}, bf16[64,8192]{1,0:T(8,128)(2,1)}, u32[]{:S(2)}) copy-start(bf16[64,8192]{1,0:T(8,128)(2,1)} %copy-done.1) | copy-start | bytes 3145732
  283.3 16.2 %copy-start.3 = (bf16[2,512,512]{2,1,0:T(8,128)(2,1)S(1)}, bf16[2,512,512]{2,1,0:T(8,128)(2,1)}, u32[]{:S(2)}) copy-start(bf16[2,512,512]{2,1,0:T(8,128)(2,1)} %param.5) | copy-start | bytes 3145732
Sparse Core Ops, SparseCore 0:
  160.8 20.3 reduce-scatter.2
  309.6 17.3 reduce-scatter.4
where the time goes:
time: 339 us; the launch traced here: 335 us
  local copies, waits for them, and re-layouts  173 us (51%)
  matrix products  75.4 us (22%)
  waiting for transfers between devices  38 us (11%)
  blocking collectives  31.2 us (9%)
  between operations  13.6 us (4%)
  other arithmetic  4.46 us (1%)
    reshape x4, local copies, waits for them, and re-layouts, pair_self_energy(): right_prod.reshape(2, pair_count, orbitals, aux_count, orbitals)  84.8 us
    reshape x2, local copies, waits for them, and re-layouts, pair_self_energy(): left_prod = left_prod.reshape(aux_count, orbitals, 2, pair_count, orbitals)  47.1 us
    reduce_scatter x2, waiting for transfers between devices, local(): lax.psum_scatter(shuffled.astype(jnp.bfloat16), 'row', scatter_dimension=...  37.9 us
    dot_general x2, matrix products, pair_self_energy(): jnp.einsum('npq,qm->npm', bubble, fit_vectors, preferred_element_type=jnp...  29.7 us
    dot_general x2, matrix products, pair_self_energy(): jnp.einsum('picnl,nplj->cnij', left_prod, screened, preferred_element_typ...  20.2 us
    all_to_all x2, blocking collectives, local(): lax.all_to_all(shaped.astype(jnp.bfloat16), 'col', split_axis=4, concat_a...  18.2 us
    all_gather x2, blocking collectives, local(): segment = lax.all_gather(self_energy, 'col', axis=2, tiled=True)  13.1 us
    convert_element_type x2, local copies, waits for them, and re-layouts, pair_self_energy(): screened = jnp.einsum('npq,qm->npm', bubble, fit_vectors, preferred_eleme...  12.7 us
  transfers between devices with their start and end apart: 2, of which 2 were waited for; matrix products, arithmetic and copies ran while one was open for 0% of the time, Pallas kernels for 0%

commit v1 on v0

v1 whole, which is shorter than its diff:
```python
import functools

import jax
import jax.numpy as jnp
from jax import lax
from jax.experimental import pallas as pl
from jax.experimental.pallas import tpu as pltpu
from jax.sharding import PartitionSpec as P

NO = 64
NEW = 2
ITERS = 2
PITCH = NO + 8
F32 = jnp.float32
BF16 = jnp.bfloat16
MESH = pl.DeviceIdType.MESH
VMEM = pl.BlockSpec(memory_space=pltpu.VMEM)


def mm(a, b):
    return jnp.dot(a, b, preferred_element_type=F32)


def mm_nt(a, b):
    return lax.dot_general(a, b, (((1,), (1,)), ((), ())), preferred_element_type=F32)


def prep_kernel(fit_ref, inner_ref, outer_ref, turned):
    aux = fit_ref.shape[0]
    for pair in range(NO // 2):
        block = fit_ref[:, pair * 2 * NO : (pair + 1) * 2 * NO].astype(F32).T
        for half in range(2):
            i = 2 * pair + half
            piece = block[half * NO : (half + 1) * NO]
            inner_ref[:, i * aux : (i + 1) * aux] = piece.astype(BF16)
            turned[i * PITCH : i * PITCH + NO, :] = piece
    for j in range(NO):
        piece = turned[pl.ds(j, NO, stride=PITCH), :]
        outer_ref[j * aux : (j + 1) * aux, :] = piece.T.astype(BF16)


def energy_kernel(green_ref, fit_ref, inner_ref, outer_ref, energy_ref, g_in, g_out, spread, m_ref, k_ref, pi_ref, w_ref):
    aux = fit_ref.shape[0]
    times = green_ref.shape[2] // NO
    pairs = NEW * times
    width = 2 * NO
    for c in range(2):
        block = green_ref[c]
        block_t = block.T
        for a in range(NEW):
            for k in range(times):
                at = ((a * times + k) * 2 + c) * NO
                g_out[at : at + NO, :] = block[a * NO : (a + 1) * NO, k * NO : (k + 1) * NO].astype(BF16)
                g_in[at : at + NO, :] = block_t[k * NO : (k + 1) * NO, a * NO : (a + 1) * NO].astype(BF16)

    rows = pairs * width

    def left(step, carry):
        lanes = pl.ds(pl.multiple_of(step * 2 * aux, 2 * aux), 2 * aux)
        res = mm(g_in[...], inner_ref[:, lanes])
        spread[pl.ds(2 * step, rows, stride=PITCH), :] = res[:, :aux]
        spread[pl.ds(2 * step + 1, rows, stride=PITCH), :] = res[:, aux:]
        return carry

    lax.fori_loop(0, NO // 2, left, 0)

    def right(step, carry):
        at = pl.ds(pl.multiple_of(step * aux, aux), aux)
        k_ref[at, :] = mm_nt(outer_ref[at, :], g_out[...]).astype(BF16)
        return carry

    lax.fori_loop(0, NO, right, 0)

    for n in range(pairs):

        def bubble(step, acc):
            lhs, rhs = [], []
            for d in range(2):
                m = 2 * step + d
                for c in range(2):
                    at = pl.multiple_of(((n * 2 + c) * NO + m) * PITCH, 8)
                    rhs.append(spread[pl.ds(at, NO), :].astype(BF16))
                m_ref[n * NO + m] = jnp.concatenate(rhs[-2:], axis=0)
                lhs.append(k_ref[pl.ds(pl.multiple_of(m * aux, aux), aux), n * width : (n + 1) * width])
            return acc + mm(jnp.concatenate(lhs, axis=1), jnp.concatenate(rhs, axis=0))

        acc = lax.fori_loop(0, NO // 2, bubble, jnp.zeros((aux, aux), F32), unroll=4)
        pi_ref[n * aux : (n + 1) * aux, :] = (acc.T * (1.0 / NO)).astype(BF16)

    def screen(step, carry):
        lanes = pl.ds(pl.multiple_of(step * 256, 256), 256)
        w_ref[:, lanes] = mm(pi_ref[...], fit_ref[:, lanes]).astype(BF16)
        return carry

    lax.fori_loop(0, NO * NO // 256, screen, 0)

    scale = (aux * NO) ** (-0.5)
    for a in range(NEW):
        outs = []
        for k in range(times):
            n = a * times + k

            def final(step, acc):
                at = n * NO + 4 * step
                even = jnp.concatenate([m_ref[at], m_ref[at + 2]], axis=1)
                odd = jnp.concatenate([m_ref[at + 1], m_ref[at + 3]], axis=1)
                w = [
                    w_ref[n * aux : (n + 1) * aux, pl.ds(pl.multiple_of((2 * step + d) * width, width), width)]
                    for d in range(2)
                ]
                return acc + mm(jnp.concatenate([even, odd], axis=0), jnp.concatenate(w, axis=0))

            acc = lax.fori_loop(0, NO // 4, final, jnp.zeros((2 * width, width), F32), unroll=2)
            outs.append((acc[:width, :NO] + acc[width:, NO:]) * scale)
        whole = jnp.concatenate(outs, axis=1).astype(BF16)
        for c in range(2):
            at = (c * NEW + a) * NO
            energy_ref[at : at + NO, :] = whole[c * NO : (c + 1) * NO]


def collide_kernel(rows_n, cols_n, energy_ref, start_ref, hist_ref, out_ref, seg, part, got, gs_sem, gr_sem, ss_sem, sr_sem):
    row, col = lax.axis_index("row"), lax.axis_index("col")
    span = energy_ref.shape[1]
    half = energy_ref.shape[0] // 2
    mine = row * cols_n + col
    source_col = mine // rows_n

    def owner(m):
        t = col * rows_n + m
        return t // cols_n, lax.rem(t, cols_n)

    barrier = pltpu.get_barrier_semaphore()
    for d in range(1, cols_n):
        pl.semaphore_signal(
            barrier, inc=1, device_id={"row": row, "col": lax.rem(col + d, cols_n)}, device_id_type=MESH
        )
    for r in range(rows_n):

        @pl.when(jnp.logical_or(row != r, col != source_col))
        def _():
            pl.semaphore_signal(barrier, inc=1, device_id={"row": r, "col": source_col}, device_id_type=MESH)

    keeps = jnp.where(source_col == col, 1, 0)
    pl.semaphore_wait(barrier, cols_n - 1 + rows_n - keeps)

    def gather(d):
        return pltpu.make_async_remote_copy(
            src_ref=energy_ref,
            dst_ref=seg.at[col],
            send_sem=gs_sem.at[d],
            recv_sem=gr_sem.at[d],
            device_id={"row": row, "col": lax.rem(col + d, cols_n)},
            device_id_type=MESH,
        )

    sends = [gather(d) for d in range(1, cols_n)]
    for copy in sends:
        copy.start()
    seg[col] = energy_ref[...]
    for copy in sends:
        copy.wait_recv()
    real = [seg[s, :half, :] for s in range(cols_n)]
    imag = [seg[s, half:, :] for s in range(cols_n)]
    lhs = jnp.concatenate(
        [jnp.concatenate(real + [-x for x in imag], axis=1), jnp.concatenate(imag + real, axis=1)], axis=0
    )

    def scatter(m):
        to_row, to_col = owner(m)
        return pltpu.make_async_remote_copy(
            src_ref=part.at[m],
            dst_ref=got.at[row],
            send_sem=ss_sem.at[m],
            recv_sem=sr_sem.at[row],
            device_id={"row": to_row, "col": to_col},
            device_id_type=MESH,
        )

    def away(m):
        to_row, to_col = owner(m)
        return jnp.logical_or(to_row != row, to_col != col)

    for m in range(rows_n):
        value = mm(lhs, hist_ref[:, m * span : (m + 1) * span]).astype(BF16)
        part[m] = value

        @pl.when(away(m))
        def _():
            scatter(m).start()

        @pl.when(jnp.logical_not(away(m)))
        def _():
            got[row] = value

    for r in range(rows_n):

        @pl.when(jnp.logical_or(row != r, col != source_col))
        def _():
            pltpu.make_async_remote_copy(
                src_ref=part.at[r],
                dst_ref=got.at[r],
                send_sem=ss_sem.at[r],
                recv_sem=sr_sem.at[r],
                device_id={"row": r, "col": source_col},
                device_id_type=MESH,
            ).wait_recv()

    total = got[0].astype(F32)
    for r in range(1, rows_n):
        total = total + got[r].astype(F32)
    out_ref[...] = start_ref[...] + total
    for copy in sends:
        copy.wait_send()
    for m in range(rows_n):

        @pl.when(away(m))
        def _():
            scatter(m).wait_send()


def local(green, fit, history):
    rows_n, cols_n = lax.axis_size("row"), lax.axis_size("col")
    aux = fit.shape[0]
    slice_rows, span = green.shape[1], green.shape[2]
    pairs = NEW * (span // NO)
    wide = pltpu.CompilerParams(vmem_limit_bytes=62 << 20)
    inner, outer = pl.pallas_call(
        prep_kernel,
        out_shape=(
            jax.ShapeDtypeStruct((NO, NO * aux), BF16),
            jax.ShapeDtypeStruct((NO * aux, NO), BF16),
        ),
        in_specs=[VMEM],
        out_specs=(VMEM, VMEM),
        scratch_shapes=[pltpu.VMEM((NO * PITCH, aux), F32)],
        name="prep",
    )(fit)
    energy = pl.pallas_call(
        energy_kernel,
        out_shape=jax.ShapeDtypeStruct((2 * slice_rows, span), BF16),
        in_specs=[VMEM] * 4,
        out_specs=VMEM,
        scratch_shapes=[
            pltpu.VMEM((pairs * 2 * NO, NO), BF16),
            pltpu.VMEM((pairs * 2 * NO, NO), BF16),
            pltpu.VMEM((pairs * 2 * NO * PITCH, aux), F32),
            pltpu.VMEM((pairs * NO, 2 * NO, aux), BF16),
            pltpu.VMEM((NO * aux, pairs * 2 * NO), BF16),
            pltpu.VMEM((pairs * aux, aux), BF16),
            pltpu.VMEM((pairs * aux, NO * NO), BF16),
        ],
        compiler_params=wide,
        name="energy",
    )
    collide = pl.pallas_call(
        functools.partial(collide_kernel, rows_n, cols_n),
        out_shape=jax.ShapeDtypeStruct((2 * slice_rows, span), F32),
        in_specs=[VMEM] * 3,
        out_specs=VMEM,
        scratch_shapes=[
            pltpu.VMEM((cols_n, 2 * slice_rows, span), BF16),
            pltpu.VMEM((rows_n, 2 * slice_rows, span), BF16),
            pltpu.VMEM((rows_n, 2 * slice_rows, span), BF16),
            pltpu.SemaphoreType.DMA((cols_n,)),
            pltpu.SemaphoreType.DMA((cols_n,)),
            pltpu.SemaphoreType.DMA((rows_n,)),
            pltpu.SemaphoreType.DMA((rows_n,)),
        ],
        compiler_params=pltpu.CompilerParams(
            collective_id=0, has_side_effects=True, vmem_limit_bytes=62 << 20
        ),
        name="collide",
    )
    start = green.reshape(2 * slice_rows, span)
    stacked = history.reshape(2 * history.shape[1], history.shape[2])
    current = start
    for _ in range(ITERS):
        sigma = energy(current.reshape(green.shape), fit, inner, outer)
        current = collide(sigma, start, stacked)
    return current.reshape(green.shape)


def solution(mesh):
    in_specs = (P("groups", None, ("row", "col")), P("groups", None), P("groups", "row", "col"))
    out_specs = P("groups", None, ("row", "col"))
    return jax.shard_map(local, mesh=mesh, in_specs=in_specs, out_specs=out_specs, check_vma=False)
```

time: 339 us -> 131 us (0.39)
  the two profiles are of different devices: /device:TPU:0 before, /device:TPU:7 now
where the time goes in v1:
time: 131 us
  Pallas kernels  130 us (99%)
  local copies, waits for them, and re-layouts  1.57 us (1%)
    pallas_call x2, Pallas kernels, local(): sigma = energy(current.reshape(green.shape), fit, inner, outer)  83.2 us
    pallas_call x2, Pallas kernels, local(): current = collide(sigma, start, stacked)  42.9 us
    pallas_call x1, Pallas kernels, local(): pl.pallas_call(prep_kernel, out_shape=(jax.ShapeDtypeStruct((NO, NO * aux...  3.51 us

profile of v1, /device:TPU:7, one launch (start us, length us, event | category | flops | bytes accessed | tf_op | source)
XLA Modules:
  0.0 131.2 jit_solution(12108035882530786209)
XLA Ops:
  0.0 3.5 %prep.1 = (bf16[64,8192]{1,0:T(8,128)(2,1)}, bf16[8192,64]{1,0:T(8,128)(2,1)}) custom-call(bf16[128,4096]{1,0:T(8,128)(2,1)} %fit_ref.5), custom_call_target="tpu_custom_call" | custom-call | tf_op jit(solution)/shard_map/prep/pallas_call | solution.py:227
  3.5 41.6 %energy.2.energy_ref = bf16[256,128]{1,0:T(8,128)(2,1)} custom-call(f32[2,128,128]{2,1,0:T(8,128)} %green_ref.1, bf16[128,4096]{1,0:T(8,128)(2,1)} %fit_ref.5, bf16[64,8192]{1,0:T(8,128)(2,1)} %get-tuple-element.7.inner_ref, bf16[8192,64]{1,0:T(8,128)(2,1)} %get-tuple-element.8.outer_ref), custom_call_target="tpu_custom_call" | custom-call | tf_op jit(solution)/shard_map/energy/pallas_call | solution.py:278
  45.1 23.1 %collide.2 = f32[256,128]{1,0:T(8,128)} custom-call(bf16[256,128]{1,0:T(8,128)(2,1)} %energy.2.energy_ref, f32[256,128]{1,0:T(8,128)} %bitcast.6, bf16[1024,512]{1,0:T(8,128)(2,1)} %bitcast.4), custom_call_target="tpu_custom_call" | custom-call | tf_op jit(solution)/shard_map/collide/pallas_call | solution.py:279
  68.2 41.6 %energy.3.energy_ref = bf16[256,128]{1,0:T(8,128)(2,1)} custom-call(f32[2,128,128]{2,1,0:T(8,128)} %bitcast.8, bf16[128,4096]{1,0:T(8,128)(2,1)} %fit_ref.5, bf16[64,8192]{1,0:T(8,128)(2,1)} %get-tuple-element.7.inner_ref, bf16[8192,64]{1,0:T(8,128)(2,1)} %get-tuple-element.8.outer_ref), custom_call_target="tpu_custom_call" | custom-call | tf_op jit(solution)/shard_map/energy/pallas_call | solution.py:278
  109.8 19.8 %collide.3 = f32[256,128]{1,0:T(8,128)} custom-call(bf16[256,128]{1,0:T(8,128)(2,1)} %energy.3.energy_ref, f32[256,128]{1,0:T(8,128)} %bitcast.7, bf16[1024,512]{1,0:T(8,128)(2,1)} %bitcast.5), custom_call_target="tpu_custom_call" | custom-call | tf_op jit(solution)/shard_map/collide/pallas_call | solution.py:279
  129.6 1.6 %copy.5 = f32[2,128,128]{2,1,0:T(8,128)} copy(f32[2,128,128]{2,1,0:T(8,128)} %bitcast.9) | data formatting | bytes 262144

commit v2 on v1

--- a/solution.py
+++ b/solution.py
@@ -11,6 +11,8 @@
 NEW = 2
 ITERS = 2
 PITCH = NO + 8
+UL, UR, UB, US, UF = 16, 4, 2, 16, 2
+RB, BB, FB = 16, 32, 16
 F32 = jnp.float32
 BF16 = jnp.bfloat16
 MESH = pl.DeviceIdType.MESH
@@ -62,21 +64,21 @@
         spread[pl.ds(2 * step + 1, rows, stride=PITCH), :] = res[:, aux:]
         return carry
 
-    lax.fori_loop(0, NO // 2, left, 0)
+    lax.fori_loop(0, NO // 2, left, 0, unroll=UL)
 
     def right(step, carry):
-        at = pl.ds(pl.multiple_of(step * aux, aux), aux)
+        at = pl.ds(pl.multiple_of(step * RB * aux, aux), RB * aux)
         k_ref[at, :] = mm_nt(outer_ref[at, :], g_out[...]).astype(BF16)
         return carry
 
-    lax.fori_loop(0, NO, right, 0)
+    lax.fori_loop(0, NO // RB, right, 0, unroll=UR)
 
     for n in range(pairs):
 
         def bubble(step, acc):
             lhs, rhs = [], []
-            for d in range(2):
-                m = 2 * step + d
+            for d in range(BB):
+                m = BB * step + d
                 for c in range(2):
                     at = pl.multiple_of(((n * 2 + c) * NO + m) * PITCH, 8)
                     rhs.append(spread[pl.ds(at, NO), :].astype(BF16))
@@ -84,7 +86,7 @@
                 lhs.append(k_ref[pl.ds(pl.multiple_of(m * aux, aux), aux), n * width : (n + 1) * width])
             return acc + mm(jnp.concatenate(lhs, axis=1), jnp.concatenate(rhs, axis=0))
 
-        acc = lax.fori_loop(0, NO // 2, bubble, jnp.zeros((aux, aux), F32), unroll=4)
+        acc = lax.fori_loop(0, NO // BB, bubble, jnp.zeros((aux, aux), F32), unroll=UB)
         pi_ref[n * aux : (n + 1) * aux, :] = (acc.T * (1.0 / NO)).astype(BF16)
 
     def screen(step, carry):
@@ -92,7 +94,7 @@
         w_ref[:, lanes] = mm(pi_ref[...], fit_ref[:, lanes]).astype(BF16)
         return carry
 
-    lax.fori_loop(0, NO * NO // 256, screen, 0)
+    lax.fori_loop(0, NO * NO // 256, screen, 0, unroll=US)
 
     scale = (aux * NO) ** (-0.5)
     for a in range(NEW):
@@ -101,16 +103,16 @@
             n = a * times + k
 
             def final(step, acc):
-                at = n * NO + 4 * step
-                even = jnp.concatenate([m_ref[at], m_ref[at + 2]], axis=1)
-                odd = jnp.concatenate([m_ref[at + 1], m_ref[at + 3]], axis=1)
+                at = n * NO + 2 * FB * step
+                even = jnp.concatenate([m_ref[at + 2 * d] for d in range(FB)], axis=1)
+                odd = jnp.concatenate([m_ref[at + 2 * d + 1] for d in range(FB)], axis=1)
                 w = [
-                    w_ref[n * aux : (n + 1) * aux, pl.ds(pl.multiple_of((2 * step + d) * width, width), width)]
-                    for d in range(2)
+                    w_ref[n * aux : (n + 1) * aux, pl.ds(pl.multiple_of((FB * step + d) * width, width), width)]
+                    for d in range(FB)
                 ]
                 return acc + mm(jnp.concatenate([even, odd], axis=0), jnp.concatenate(w, axis=0))
 
-            acc = lax.fori_loop(0, NO // 4, final, jnp.zeros((2 * width, width), F32), unroll=2)
+            acc = lax.fori_loop(0, NO // (2 * FB), final, jnp.zeros((2 * width, width), F32), unroll=UF)
             outs.append((acc[:width, :NO] + acc[width:, NO:]) * scale)
         whole = jnp.concatenate(outs, axis=1).astype(BF16)
         for c in range(2):

time: 131 us -> 77.1 us (0.59)
  Pallas kernels: 130 us -> 75.3 us
    pallas_call x2, Pallas kernels: 83.2 us -> 28.9 us  [local(): sigma = energy(current.reshape(green.shape), fit, inner, outer)]
where the time goes in v2:
time: 77.1 us; the launch traced here: 76.9 us
  Pallas kernels  75.3 us (98%)
  local copies, waits for them, and re-layouts  1.57 us (2%)
    pallas_call x2, Pallas kernels, local(): current = collide(sigma, start, stacked)  42.9 us
    pallas_call x2, Pallas kernels, local(): sigma = energy(current.reshape(green.shape), fit, inner, outer)  28.9 us
    pallas_call x1, Pallas kernels, local(): pl.pallas_call(prep_kernel, out_shape=(jax.ShapeDtypeStruct((NO, NO * aux...  3.51 us
    unnamed x1, local copies, waits for them, and re-layouts  1.57 us

profile of v2, /device:TPU:7, one launch (start us, length us, event | category | flops | bytes accessed | tf_op | source)
XLA Modules:
  0.0 76.9 jit_solution(2273790943933010881)
XLA Ops:
  0.0 3.5 %prep.1 = (bf16[64,8192]{1,0:T(8,128)(2,1)}, bf16[8192,64]{1,0:T(8,128)(2,1)}) custom-call(bf16[128,4096]{1,0:T(8,128)(2,1)} %fit_ref.5), custom_call_target="tpu_custom_call" | custom-call | tf_op jit(solution)/shard_map/prep/pallas_call | solution.py:229
  3.5 14.5 %energy.2.energy_ref = bf16[256,128]{1,0:T(8,128)(2,1)} custom-call(f32[2,128,128]{2,1,0:T(8,128)} %green_ref.1, bf16[128,4096]{1,0:T(8,128)(2,1)} %fit_ref.5, bf16[64,8192]{1,0:T(8,128)(2,1)} %get-tuple-element.7.inner_ref, bf16[8192,64]{1,0:T(8,128)(2,1)} %get-tuple-element.8.outer_ref), custom_call_target="tpu_custom_call" | custom-call | tf_op jit(solution)/shard_map/energy/pallas_call | solution.py:280
  18.0 23.1 %collide.2 = f32[256,128]{1,0:T(8,128)} custom-call(bf16[256,128]{1,0:T(8,128)(2,1)} %energy.2.energy_ref, f32[256,128]{1,0:T(8,128)} %bitcast.6, bf16[1024,512]{1,0:T(8,128)(2,1)} %bitcast.4), custom_call_target="tpu_custom_call" | custom-call | tf_op jit(solution)/shard_map/collide/pallas_call | solution.py:281
  41.1 14.5 %energy.3.energy_ref = bf16[256,128]{1,0:T(8,128)(2,1)} custom-call(f32[2,128,128]{2,1,0:T(8,128)} %bitcast.8, bf16[128,4096]{1,0:T(8,128)(2,1)} %fit_ref.5, bf16[64,8192]{1,0:T(8,128)(2,1)} %get-tuple-element.7.inner_ref, bf16[8192,64]{1,0:T(8,128)(2,1)} %get-tuple-element.8.outer_ref), custom_call_target="tpu_custom_call" | custom-call | tf_op jit(solution)/shard_map/energy/pallas_call | solution.py:280
  55.6 19.8 %collide.3 = f32[256,128]{1,0:T(8,128)} custom-call(bf16[256,128]{1,0:T(8,128)(2,1)} %energy.3.energy_ref, f32[256,128]{1,0:T(8,128)} %bitcast.7, bf16[1024,512]{1,0:T(8,128)(2,1)} %bitcast.5), custom_call_target="tpu_custom_call" | custom-call | tf_op jit(solution)/shard_map/collide/pallas_call | solution.py:281
  75.3 1.6 %copy.5 = f32[2,128,128]{2,1,0:T(8,128)} copy(f32[2,128,128]{2,1,0:T(8,128)} %bitcast.9) | data formatting | bytes 262144

commit v3 on v2

v3 whole, which is shorter than its diff:
```python
import functools

import jax
import jax.numpy as jnp
from jax import lax
from jax.experimental import pallas as pl
from jax.experimental.pallas import tpu as pltpu
from jax.sharding import PartitionSpec as P

NO = 64
NEW = 2
ITERS = 2
PITCH = NO + 8
UL, UR, UB, US, UF = 16, 4, 2, 16, 2
RB, BB, FB = 16, 32, 16
F32 = jnp.float32
BF16 = jnp.bfloat16
MESH = pl.DeviceIdType.MESH
VMEM = pl.BlockSpec(memory_space=pltpu.VMEM)


def mm(a, b):
    return jnp.dot(a, b, preferred_element_type=F32)


def mm_nt(a, b):
    return lax.dot_general(a, b, (((1,), (1,)), ((), ())), preferred_element_type=F32)


def prepare(fit_ref, inner_ref, outer_ref, turned):
    aux = fit_ref.shape[0]
    for pair in range(NO // 2):
        block = fit_ref[:, pair * 2 * NO : (pair + 1) * 2 * NO].astype(F32).T
        for half in range(2):
            i = 2 * pair + half
            piece = block[half * NO : (half + 1) * NO]
            inner_ref[:, i * aux : (i + 1) * aux] = piece.astype(BF16)
            turned[i * PITCH : i * PITCH + NO, :] = piece
    for j in range(NO):
        piece = turned[pl.ds(j, NO, stride=PITCH), :]
        outer_ref[j * aux : (j + 1) * aux, :] = piece.T.astype(BF16)


def products(a, now_ref, inner_ref, outer_ref, g_in, g_out, spread, k_ref):
    aux = inner_ref.shape[1] // NO
    times = now_ref.shape[2] // NO
    rows = times * 2 * NO
    for c in range(2):
        block = now_ref[c, a * NO : (a + 1) * NO, :]
        block_t = block.T
        for n in range(times):
            at = (n * 2 + c) * NO
            g_out[at : at + NO, :] = block[:, n * NO : (n + 1) * NO].astype(BF16)
            g_in[at : at + NO, :] = block_t[n * NO : (n + 1) * NO, :].astype(BF16)

    def left(step, carry):
        lanes = pl.ds(pl.multiple_of(step * 2 * aux, 2 * aux), 2 * aux)
        res = mm(g_in[...], inner_ref[:, lanes])
        spread[pl.ds(2 * step, rows, stride=PITCH), :] = res[:, :aux]
        spread[pl.ds(2 * step + 1, rows, stride=PITCH), :] = res[:, aux:]
        return carry

    lax.fori_loop(0, NO // 2, left, 0, unroll=UL)

    def right(step, carry):
        at = pl.ds(pl.multiple_of(step * RB * aux, aux), RB * aux)
        k_ref[at, :] = mm_nt(outer_ref[at, :], g_out[...]).astype(BF16)
        return carry

    lax.fori_loop(0, NO // RB, right, 0, unroll=UR)


def contract(times, fit_ref, spread, m_ref, k_ref, pi_ref, w_ref):
    aux = fit_ref.shape[0]
    width = 2 * NO
    for n in range(times):

        def bubble(step, acc):
            lhs, rhs = [], []
            for d in range(BB):
                m = BB * step + d
                for c in range(2):
                    at = pl.multiple_of(((n * 2 + c) * NO + m) * PITCH, 8)
                    rhs.append(spread[pl.ds(at, NO), :].astype(BF16))
                m_ref[n * NO + m] = jnp.concatenate(rhs[-2:], axis=0)
                lhs.append(k_ref[pl.ds(pl.multiple_of(m * aux, aux), aux), n * width : (n + 1) * width])
            return acc + mm(jnp.concatenate(lhs, axis=1), jnp.concatenate(rhs, axis=0))

        acc = lax.fori_loop(0, NO // BB, bubble, jnp.zeros((aux, aux), F32), unroll=UB)
        pi_ref[n * aux : (n + 1) * aux, :] = (acc.T * (1.0 / NO)).astype(BF16)

    def screen(step, carry):
        lanes = pl.ds(pl.multiple_of(step * 256, 256), 256)
        w_ref[:, lanes] = mm(pi_ref[...], fit_ref[:, lanes]).astype(BF16)
        return carry

    lax.fori_loop(0, NO * NO // 256, screen, 0, unroll=US)

    scale = (aux * NO) ** (-0.5)
    outs = []
    for n in range(times):

        def final(step, acc):
            at = n * NO + 2 * FB * step
            even = jnp.concatenate([m_ref[at + 2 * d] for d in range(FB)], axis=1)
            odd = jnp.concatenate([m_ref[at + 2 * d + 1] for d in range(FB)], axis=1)
            w = [
                w_ref[n * aux : (n + 1) * aux, pl.ds(pl.multiple_of((FB * step + d) * width, width), width)]
                for d in range(FB)
            ]
            return acc + mm(jnp.concatenate([even, odd], axis=0), jnp.concatenate(w, axis=0))

        acc = lax.fori_loop(0, NO // (2 * FB), final, jnp.zeros((2 * width, width), F32), unroll=UF)
        outs.append((acc[:width, :NO] + acc[width:, NO:]) * scale)
    return jnp.concatenate(outs, axis=1).astype(BF16)


def whole_kernel(
    rows_n, cols_n, green_ref, fit_ref, hist_ref, out_ref,
    inner, outer, turned, g_in, g_out, spread, m_ref, k_ref, pi_ref, w_ref,
    now, energy, seg, part, got, gs_sem, gr_sem, ss_sem, sr_sem,
):
    row, col = lax.axis_index("row"), lax.axis_index("col")
    span = green_ref.shape[2]
    times = span // NO
    source_col = (row * cols_n + col) // rows_n

    def owner(m):
        t = col * rows_n + m
        return t // cols_n, lax.rem(t, cols_n)

    def away(m):
        to_row, to_col = owner(m)
        return jnp.logical_or(to_row != row, to_col != col)

    def foreign(r):
        return jnp.logical_or(row != r, col != source_col)

    def place(r, c):
        return {"row": r, "col": c}

    barrier = pltpu.get_barrier_semaphore()
    for d in range(1, cols_n):
        pl.semaphore_signal(barrier, inc=1, device_id=place(row, lax.rem(col + d, cols_n)), device_id_type=MESH)
    for r in range(rows_n):

        @pl.when(foreign(r))
        def _():
            pl.semaphore_signal(barrier, inc=1, device_id=place(r, source_col), device_id_type=MESH)

    prepare(fit_ref, inner, outer, turned)

    keeps = jnp.where(source_col == col, 1, 0)
    pl.semaphore_wait(barrier, cols_n - 1 + rows_n - keeps)

    def gather(s, d):
        return pltpu.make_async_remote_copy(
            src_ref=energy.at[s],
            dst_ref=seg.at[s, col],
            send_sem=gs_sem.at[s, d],
            recv_sem=gr_sem.at[s, d],
            device_id=place(row, lax.rem(col + d, cols_n)),
            device_id_type=MESH,
        )

    def scatter(s, m):
        return pltpu.make_async_remote_copy(
            src_ref=part.at[s, m],
            dst_ref=got.at[s, row],
            send_sem=ss_sem.at[s, m],
            recv_sem=sr_sem.at[s, row],
            device_id=place(*owner(m)),
            device_id_type=MESH,
        )

    def arriving(s, r):
        return pltpu.make_async_remote_copy(
            src_ref=part.at[s, r],
            dst_ref=got.at[s, r],
            send_sem=ss_sem.at[s, r],
            recv_sem=sr_sem.at[s, r],
            device_id=place(r, source_col),
            device_id_type=MESH,
        )

    def multiply(s):
        for d in range(1, cols_n):
            gather(s, d).wait_recv()
        real = [seg[s, q, :NO, :] for q in range(cols_n)]
        imag = [seg[s, q, NO:, :] for q in range(cols_n)]
        lhs = jnp.concatenate(
            [jnp.concatenate(real + [-x for x in imag], axis=1), jnp.concatenate(imag + real, axis=1)], axis=0
        )
        for m in range(rows_n):
            value = mm(lhs, hist_ref[:, m * span : (m + 1) * span]).astype(BF16)
            part[s, m] = value

            @pl.when(away(m))
            def _():
                scatter(s, m).start()

            @pl.when(jnp.logical_not(away(m)))
            def _():
                got[s, row] = value

    def collect(s, target):
        a = s % NEW
        for r in range(rows_n):

            @pl.when(foreign(r))
            def _():
                arriving(s, r).wait_recv()

        total = got[s, 0].astype(F32)
        for r in range(1, rows_n):
            total = total + got[s, r].astype(F32)
        for c in range(2):
            at = slice(a * NO, (a + 1) * NO)
            target[c, at, :] = green_ref[c, at, :] + total[c * NO : (c + 1) * NO]

    steps = ITERS * NEW
    for s in range(steps):
        a = s % NEW
        if s >= NEW:
            collect(s - NEW, now)
        products(a, green_ref if s < NEW else now, inner, outer, g_in, g_out, spread, k_ref)
        if s >= 1:
            multiply(s - 1)
        value = contract(times, fit_ref, spread, m_ref, k_ref, pi_ref, w_ref)
        energy[s] = value
        for d in range(1, cols_n):
            gather(s, d).start()
        seg[s, col] = value
    multiply(steps - 1)
    for s in range(steps - NEW, steps):
        collect(s, out_ref)
    for s in range(steps):
        for d in range(1, cols_n):
            gather(s, d).wait_send()
        for m in range(rows_n):

            @pl.when(away(m))
            def _():
                scatter(s, m).wait_send()


def local(green, fit, history):
    rows_n, cols_n = lax.axis_size("row"), lax.axis_size("col")
    aux = fit.shape[0]
    span = green.shape[2]
    times = span // NO
    steps = ITERS * NEW
    stacked = history.reshape(2 * history.shape[1], history.shape[2])
    block = (2 * NO, span)
    return pl.pallas_call(
        functools.partial(whole_kernel, rows_n, cols_n),
        out_shape=jax.ShapeDtypeStruct(green.shape, F32),
        in_specs=[VMEM] * 3,
        out_specs=VMEM,
        scratch_shapes=[
            pltpu.VMEM((NO, NO * aux), BF16),
            pltpu.VMEM((NO * aux, NO), BF16),
            pltpu.VMEM((NO * PITCH, aux), F32),
            pltpu.VMEM((times * 2 * NO, NO), BF16),
            pltpu.VMEM((times * 2 * NO, NO), BF16),
            pltpu.VMEM((times * 2 * NO * PITCH, aux), F32),
            pltpu.VMEM((times * NO, 2 * NO, aux), BF16),
            pltpu.VMEM((NO * aux, times * 2 * NO), BF16),
            pltpu.VMEM((times * aux, aux), BF16),
            pltpu.VMEM((times * aux, NO * NO), BF16),
            pltpu.VMEM(green.shape, F32),
            pltpu.VMEM((steps, *block), BF16),
            pltpu.VMEM((steps, cols_n, *block), BF16),
            pltpu.VMEM((steps, rows_n, *block), BF16),
            pltpu.VMEM((steps, rows_n, *block), BF16),
            pltpu.SemaphoreType.DMA((steps, cols_n)),
            pltpu.SemaphoreType.DMA((steps, cols_n)),
            pltpu.SemaphoreType.DMA((steps, rows_n)),
            pltpu.SemaphoreType.DMA((steps, rows_n)),
        ],
        compiler_params=pltpu.CompilerParams(
            collective_id=0, has_side_effects=True, vmem_limit_bytes=62 << 20
        ),
        name="whole",
    )(green, fit, stacked)


def solution(mesh):
    in_specs = (P("groups", None, ("row", "col")), P("groups", None), P("groups", "row", "col"))
    out_specs = P("groups", None, ("row", "col"))
    return jax.shard_map(local, mesh=mesh, in_specs=in_specs, out_specs=out_specs, check_vma=False)
```

time: 77.1 us -> 55.1 us (0.71)
  Pallas kernels: 75.3 us -> 53.4 us
    pallas_call x5 -> x1, Pallas kernels: 75.3 us -> 53.4 us  [local(): pl.pallas_call(functools.partial(whole_kernel, rows_n, cols_n), out_shape...]
where the time goes in v3:
time: 55.1 us; the launch traced here: 54.9 us
  Pallas kernels  53.4 us (97%)
  local copies, waits for them, and re-layouts  1.57 us (3%)
    pallas_call x1, Pallas kernels, local(): pl.pallas_call(functools.partial(whole_kernel, rows_n, cols_n), out_shape...  53.4 us
    unnamed x1, local copies, waits for them, and re-layouts  1.57 us

profile of v3, /device:TPU:7, one launch (start us, length us, event | category | flops | bytes accessed | tf_op | source)
XLA Modules:
  0.0 54.9 jit_solution(2022192099220060254)
XLA Ops:
  0.0 53.4 %whole.1 = f32[2,128,128]{2,1,0:T(8,128)} custom-call(f32[2,128,128]{2,1,0:T(8,128)} %green_ref.1, bf16[128,4096]{1,0:T(8,128)(2,1)} %fit_ref.1, bf16[1024,512]{1,0:T(8,128)(2,1)} %bitcast.1), custom_call_target="tpu_custom_call" | custom-call | tf_op jit(solution)/shard_map/whole/pallas_call | solution.py:255
  53.4 1.6 %copy.5 = f32[2,128,128]{2,1,0:T(8,128)} copy(f32[2,128,128]{2,1,0:T(8,128)} %whole.1) | data formatting | bytes 262144
